TPU v7x, 512 devices: a whole 4x8x8 slice. The times are simulated.
512 devices in a mesh: pipe: 16 (over y, z_lo), expert: 32 (over z_hi, x, core).
Axes of the slice: x: 4, y: 8, z: 8 (z_hi: 4, z_lo: 2; z = z_hi * 2 + z_lo), core: 2. Of those that a mesh axis runs over, the one named last changes fastest.
Arguments:
- in_flight: bfloat16 [2, 16, 512, 3584], P(None, 'pipe', 'expert'), may hold values from -6 to 6
- norm_gain: bfloat16 [2, 16, 3584], P(None, 'pipe'), may hold values from 0.099609375 to 1.8984375
- router_weight: bfloat16 [2, 16, 3584, 4], P(None, 'pipe'), may hold values from -0.09375 to 0.09375
- up_weight: bfloat16 [2, 16, 3584, 4096], P(None, 'pipe', None, 'expert'), may hold values from -0.09375 to 0.09375
- down_weight: bfloat16 [2, 16, 4096, 3584], P(None, 'pipe', 'expert'), may hold values from -0.1875 to 0.1875
- chosen_experts: int32 [1, 2, 16, 512, 2], P(None, None, 'pipe', 'expert'), may hold values from 0 to 3, all different within a row; in each aligned block of 16 rows (0 to 15, 16 to 31, ..., all dimensions but the last counted through in order) at most 14 rows name the same one
Outputs:
- final_states: bfloat16 [2, 16, 512, 3584], P(None, 'pipe', 'expert')
Inputs may be any that keep to these rules, and one draw needn't show every extreme that they name: `chosen_experts`: each token names 2 different experts; among the tokens of one device's rows of one micro-batch at one step, at most 14 name the same expert, and that most is reached.
All inputs are finite; a program needn't handle non-finite values.
Results may differ from a plain program's by a relative error of at most 0.006.
Values may be sent and summed in bfloat16 or wider, within the bound.
A program may use at most 64 MiB of HBM per device.

v0:
```python
import jax
import jax.numpy as jnp
from jax import lax
from jax.sharding import PartitionSpec as P

EXPERTS = 4


def from_behind(value, axis, by):
    size = lax.axis_size(axis)
    pairs = [(i, i + by) for i in range(size) if 0 <= i + by < size]
    return lax.ppermute(value, axis, pairs)


def section_apply(tokens, gain, router, w_up, w_down, chosen):
    device_count = lax.axis_size("expert")
    group_size = device_count // EXPERTS
    row_count = tokens.shape[0]
    width = tokens.shape[1]
    capacity = row_count * 7 // 8
    wide = tokens.astype(jnp.float32)
    scale = lax.rsqrt(jnp.mean(wide * wide, axis=-1, keepdims=True) + 1e-06)
    normed = (wide * scale * gain.astype(jnp.float32)).astype(jnp.bfloat16)
    affinity = jax.nn.sigmoid(jnp.dot(normed, router, preferred_element_type=jnp.float32))
    labels = jnp.arange(EXPERTS, dtype=jnp.int32)
    picked = jnp.sum((chosen[:, :, None] == labels[None, None, :]).astype(jnp.float32), axis=1)
    weighted = affinity * picked
    gates = weighted / jnp.sum(weighted, axis=-1, keepdims=True)
    row_ids = jnp.arange(row_count, dtype=jnp.int32)
    earlier = (row_ids[None, :] < row_ids[:, None]).astype(jnp.float32)
    before = jnp.dot(earlier, picked, precision=lax.Precision.HIGHEST)
    slot_ids = jnp.arange(capacity, dtype=jnp.float32)
    select = picked.T[:, None, :] * (before.T[:, None, :] == slot_ids[None, :, None]).astype(
        jnp.float32
    )
    packed = jnp.einsum(
        "ecr,rd->ecd", select.astype(jnp.bfloat16), normed, preferred_element_type=jnp.float32
    ).astype(jnp.bfloat16)
    outgoing = jnp.broadcast_to(packed[:, None], (EXPERTS, group_size, capacity, width)).reshape(
        device_count, capacity, width
    )
    hidden = jax.nn.silu(
        jnp.einsum(
            "skd,dh->skh",
            lax.all_to_all(outgoing, "expert", split_axis=0, concat_axis=0, tiled=True),
            w_up,
            preferred_element_type=jnp.float32,
        )
    ).astype(jnp.bfloat16)
    returned = lax.all_to_all(
        jnp.einsum("skh,hd->skd", hidden, w_down, preferred_element_type=jnp.float32).astype(
            jnp.bfloat16
        ),
        "expert",
        split_axis=0,
        concat_axis=0,
        tiled=True,
    )
    summed = jnp.sum(
        returned.reshape(EXPERTS, group_size, capacity, width).astype(jnp.float32), axis=1
    )
    moe = jnp.einsum(
        "ecr,ecd->rd", select * gates.T[:, None, :], summed, precision=lax.Precision.HIGHEST
    )
    return (wide + moe).astype(jnp.bfloat16)


def shards(in_flight, norm_gain, router_weight, up_weight, down_weight, chosen_experts):
    states = [in_flight[0, 0], in_flight[1, 0]]
    pipe_rank = lax.axis_index("pipe")
    last_rank = lax.axis_size("pipe") - 1

    def run_leg(fold_leg, tick):
        return section_apply(
            states[fold_leg],
            norm_gain[fold_leg, 0],
            router_weight[fold_leg, 0],
            up_weight[fold_leg, 0],
            down_weight[fold_leg, 0],
            chosen_experts[tick, fold_leg, 0],
        )

    tick = 0
    first_out = run_leg(0, tick)
    second_out = run_leg(1, tick)
    from_above = from_behind(first_out, "pipe", 1)
    from_below = from_behind(second_out, "pipe", -1)
    states = [
        jnp.where(pipe_rank == 0, second_out, from_above),
        jnp.where(pipe_rank == last_rank, first_out, from_below),
    ]
    return jnp.stack(states)[:, None]


def solution(mesh):
    in_specs = (
        P(None, "pipe", "expert", None),
        P(None, "pipe", None),
        P(None, "pipe", None, None),
        P(None, "pipe", None, "expert"),
        P(None, "pipe", "expert", None),
        P(None, None, "pipe", "expert", None),
    )
    out_specs = P(None, "pipe", "expert", None)
    return jax.shard_map(shards, mesh=mesh, in_specs=in_specs, out_specs=out_specs, check_vma=False)
```

profile of v0, /device:TPU:36, one launch (start us, length us, event | category | flops | bytes accessed | tf_op | source)
XLA Modules:
  0.0 396.2 jit_solution(13879072489692092811)
XLA Ops:
  0.0 0.9 convert_reduce_fusion.3
  0.9 1.1 fusion.26
  2.0 0.7 slice_bitcast_fusion.1
  2.7 0.1 fusion.83
  2.9 1.2 convolution_convert_fusion.3
  4.1 2.3 broadcast_in_dim.6
  6.3 0.0 copy-start
  6.3 13.6 %all-to-all-start = ((bf16[32,14,3584]{2,1,0:T(8,128)(2,1)}), bf16[32,14,3584]{2,1,0:T(8,128)(2,1)}, u32[]{:S(2)}, u32[]{:S(2)}) async-start(bf16[32,14,3584]{2,1,0:T(8,128)(2,1)} %bitcast.136), calls=%async_computation | async-start | bytes 7340032 | tf_op jit(solution)/shard_map/all_to_all | solution.py:45
  20.0 0.1 fusion.82
  20.1 0.0 copy-done
  20.1 0.3 convolution_convert_fusion.2
  20.4 85.0 %all-to-all-done = bf16[32,14,3584]{2,1,0:T(8,128)(2,1)} async-done(((bf16[32,14,3584]{2,1,0:T(8,128)(2,1)}), bf16[32,14,3584]{2,1,0:T(8,128)(2,1)}, u32[]{:S(2)}, u32[]{:S(2)}) %all-to-all-start) | async-done | bytes 3211296 | tf_op jit(solution)/shard_map/all_to_all | solution.py:45
  105.4 2.3 broadcast_in_dim.7
  107.7 5.3 %all-to-all-start.2 = ((bf16[32,14,3584]{2,1,0:T(8,128)(2,1)}), bf16[32,14,3584]{2,1,0:T(8,128)(2,1)}, u32[]{:S(2)}, u32[]{:S(2)}) async-start(bf16[32,14,3584]{2,1,0:T(8,128)(2,1)} %bitcast.137), calls=%async_computation.2 | async-start | bytes 7340032 | tf_op jit(solution)/shard_map/all_to_all | solution.py:45
  113.0 6.1 %convolution_convert_fusion.1 = bf16[32,14,3584]{2,0,1:T(8,128)(2,1)S(1)} fusion(bf16[2,1,128,3584]{3,2,1,0:T(8,128)(2,1)} %param.10, bf16[2,1,3584,128]{3,2,1,0:T(8,128)(2,1)} %param.9, bf16[32,14,3584]{2,1,0:T(8,128)(2,1)} %all-to-all-done), kind=kOutput, calls=%fused_computation.3 | convolution fusion | flops 823975936 | bytes 8716288 | tf_op jit(solution)/shard_map/skh,hd->skd/dot_general | solution.py:51
  119.1 3.7 copy.40
  122.8 76.1 %all-to-all-done.2 = bf16[32,14,3584]{2,1,0:T(8,128)(2,1)} async-done(((bf16[32,14,3584]{2,1,0:T(8,128)(2,1)}), bf16[32,14,3584]{2,1,0:T(8,128)(2,1)}, u32[]{:S(2)}, u32[]{:S(2)}) %all-to-all-start.2) | async-done | bytes 3211296 | tf_op jit(solution)/shard_map/all_to_all | solution.py:45
  198.9 5.3 %all-to-all-start.1 = ((bf16[32,14,3584]{2,1,0:T(8,128)(2,1)}), bf16[32,14,3584]{2,1,0:T(8,128)(2,1)}, u32[]{:S(2)}, u32[]{:S(2)}) async-start(bf16[32,14,3584]{2,1,0:T(8,128)(2,1)} %copy.40), calls=%async_computation.1 | async-start | bytes 7340032 | tf_op jit(solution)/shard_map/all_to_all | solution.py:50
  204.2 6.1 %convolution_convert_fusion = bf16[32,14,3584]{2,0,1:T(8,128)(2,1)S(1)} fusion(bf16[2,1,128,3584]{3,2,1,0:T(8,128)(2,1)} %param.10, bf16[2,1,3584,128]{3,2,1,0:T(8,128)(2,1)} %param.9, bf16[32,14,3584]{2,1,0:T(8,128)(2,1)} %all-to-all-done.2), kind=kOutput, calls=%fused_computation.2 | convolution fusion | flops 823975936 | bytes 8716288 | tf_op jit(solution)/shard_map/skh,hd->skd/dot_general | solution.py:51
  210.3 3.6 copy.46
  213.9 0.0 copy-start.1
  213.9 75.9 %all-to-all-done.1 = bf16[32,14,3584]{2,1,0:T(8,128)(2,1)} async-done(((bf16[32,14,3584]{2,1,0:T(8,128)(2,1)}), bf16[32,14,3584]{2,1,0:T(8,128)(2,1)}, u32[]{:S(2)}, u32[]{:S(2)}) %all-to-all-start.1) | async-done | bytes 3211296 | tf_op jit(solution)/shard_map/all_to_all | solution.py:50
  289.8 5.1 %all-to-all-start.3 = ((bf16[32,14,3584]{2,1,0:T(8,128)(2,1)}), bf16[32,14,3584]{2,1,0:T(8,128)(2,1)}, u32[]{:S(2)}, u32[]{:S(2)}) async-start(bf16[32,14,3584]{2,1,0:T(8,128)(2,1)} %copy.46), calls=%async_computation.3 | async-start | bytes 7340032 | tf_op jit(solution)/shard_map/all_to_all | solution.py:50
  294.9 0.0 copy-done.1
  295.0 0.2 multiply_reduce_fusion
  295.2 0.2 multiply_reduce_fusion.1
  295.5 2.7 convert_reduce_fusion.1
  298.3 0.6 fusion.2
  298.8 4.3 %collective-permute-start.1 = (bf16[16,3584]{1,0:T(8,128)(2,1)S(1)}, bf16[16,3584]{1,0:T(8,128)(2,1)S(1)}, u32[]{:S(2)}, u32[]{:S(2)}) collective-permute-start(bf16[16,3584]{1,0:T(8,128)(2,1)S(1)} %fusion.2), channel_id=1, source_target_pairs={{32,0},{64,32},{96,64},{128,96},{160,128},{192,160},{224,192},{256... | collective-permute-start | bytes 344072 | tf_op jit(solution)/shard_map/ppermute | solution.py:12
  303.1 80.2 %all-to-all-done.3 = bf16[32,14,3584]{2,1,0:T(8,128)(2,1)} async-done(((bf16[32,14,3584]{2,1,0:T(8,128)(2,1)}), bf16[32,14,3584]{2,1,0:T(8,128)(2,1)}, u32[]{:S(2)}, u32[]{:S(2)}) %all-to-all-start.3) | async-done | bytes 3211296 | tf_op jit(solution)/shard_map/all_to_all | solution.py:50
  383.3 2.7 convert_reduce_fusion
  386.1 0.6 fusion.3
  386.7 1.9 collective-permute-start
  388.6 0.0 collective-permute-done.1
  388.6 6.8 %collective-permute-done = bf16[16,3584]{1,0:T(8,128)(2,1)S(1)} collective-permute-done((bf16[16,3584]{1,0:T(8,128)(2,1)S(1)}, bf16[16,3584]{1,0:T(8,128)(2,1)S(1)}, u32[]{:S(2)}, u32[]{:S(2)}) %collective-permute-start) | collective-permute-done | bytes 114720 | tf_op jit(solution)/shard_map/ppermute | solution.py:12
  395.5 0.7 maximum_bitcast_fusion
  (10 shorter events, 0.1 us)
Async XLA Ops:
  6.3 13.8 %copy-start = (bf16[2,1,16,3584]{3,2,1,0:T(8,128)(2,1)S(1)}, bf16[2,1,16,3584]{3,2,1,0:T(8,128)(2,1)}, u32[]{:S(2)}) copy-start(bf16[2,1,16,3584]{3,2,1,0:T(8,128)(2,1)} %param.6) | copy-start | bytes 688132
  6.3 99.1 %all-to-all-start = ((bf16[32,14,3584]{2,1,0:T(8,128)(2,1)}), bf16[32,14,3584]{2,1,0:T(8,128)(2,1)}, u32[]{:S(2)}, u32[]{:S(2)}) async-start(bf16[32,14,3584]{2,1,0:T(8,128)(2,1)} %bitcast.136), calls=%async_computation | async-start | bytes 7340032 | tf_op jit(solution)/shard_map/all_to_all | solution.py:45
  107.7 91.2 %all-to-all-start.2 = ((bf16[32,14,3584]{2,1,0:T(8,128)(2,1)}), bf16[32,14,3584]{2,1,0:T(8,128)(2,1)}, u32[]{:S(2)}, u32[]{:S(2)}) async-start(bf16[32,14,3584]{2,1,0:T(8,128)(2,1)} %bitcast.137), calls=%async_computation.2 | async-start | bytes 7340032 | tf_op jit(solution)/shard_map/all_to_all | solution.py:45
  198.9 90.9 %all-to-all-start.1 = ((bf16[32,14,3584]{2,1,0:T(8,128)(2,1)}), bf16[32,14,3584]{2,1,0:T(8,128)(2,1)}, u32[]{:S(2)}, u32[]{:S(2)}) async-start(bf16[32,14,3584]{2,1,0:T(8,128)(2,1)} %copy.40), calls=%async_computation.1 | async-start | bytes 7340032 | tf_op jit(solution)/shard_map/all_to_all | solution.py:50
  213.9 81.0 %copy-start.1 = (bf16[2,1,3584,4]{2,3,1,0:T(4,128)(2,1)S(1)}, bf16[2,1,3584,4]{2,3,1,0:T(4,128)(2,1)}, u32[]{:S(2)}) copy-start(bf16[2,1,3584,4]{2,3,1,0:T(4,128)(2,1)} %param.8) | copy-start | bytes 172036
  289.8 93.5 %all-to-all-start.3 = ((bf16[32,14,3584]{2,1,0:T(8,128)(2,1)}), bf16[32,14,3584]{2,1,0:T(8,128)(2,1)}, u32[]{:S(2)}, u32[]{:S(2)}) async-start(bf16[32,14,3584]{2,1,0:T(8,128)(2,1)} %copy.46), calls=%async_computation.3 | async-start | bytes 7340032 | tf_op jit(solution)/shard_map/all_to_all | solution.py:50
  298.8 89.7 %collective-permute-start.1 = (bf16[16,3584]{1,0:T(8,128)(2,1)S(1)}, bf16[16,3584]{1,0:T(8,128)(2,1)S(1)}, u32[]{:S(2)}, u32[]{:S(2)}) collective-permute-start(bf16[16,3584]{1,0:T(8,128)(2,1)S(1)} %fusion.2), channel_id=1, source_target_pairs={{32,0},{64,32},{96,64},{128,96},{160,128},{192,160},{224,192},{256... | collective-permute-start | bytes 344072 | tf_op jit(solution)/shard_map/ppermute | solution.py:12
  386.7 8.8 %collective-permute-start = (bf16[16,3584]{1,0:T(8,128)(2,1)S(1)}, bf16[16,3584]{1,0:T(8,128)(2,1)S(1)}, u32[]{:S(2)}, u32[]{:S(2)}) collective-permute-start(bf16[16,3584]{1,0:T(8,128)(2,1)S(1)} %fusion.3), channel_id=1, source_target_pairs={{0,32},{32,64},{64,96},{96,128},{128,160},{160,192},{192,224},{224... | collective-permute-start | bytes 344072 | tf_op jit(solution)/shard_map/ppermute | solution.py:12
where the time goes:
time: 397 us; the launch traced here: 396 us
  waiting for transfers between devices  324 us (82%)
  starting transfers between devices  35.5 us (9%)
  matrix products  15.5 us (4%)
  local copies, waits for them, and re-layouts  12.6 us (3%)
  other arithmetic  8.32 us (2%)
    all_to_all x2, waiting for transfers between devices, section_apply(): lax.all_to_all(outgoing, 'expert', split_axis=0, concat_axis=0, tiled=True)  161 us
    all_to_all x2, waiting for transfers between devices, section_apply(): lax.all_to_all(jnp.einsum('skh,hd->skd', hidden, w_down, preferred_elemen...  156 us
    all_to_all x2, starting transfers between devices, section_apply(): lax.all_to_all(outgoing, 'expert', split_axis=0, concat_axis=0, tiled=True)  18.9 us
    dot_general x2, matrix products, section_apply(): jnp.einsum('skh,hd->skd', hidden, w_down, preferred_element_type=jnp.floa...  12.2 us
    all_to_all x2, starting transfers between devices, section_apply(): lax.all_to_all(jnp.einsum('skh,hd->skd', hidden, w_down, preferred_elemen...  10.4 us
  transfers between devices with their start and end apart: 6, of which 5 were waited for; matrix products, arithmetic and copies ran while one was open for 7% of the time, Pallas kernels for 0%

commit v1 on v0

v1 whole, which is shorter than its diff:
```python
import jax
import jax.numpy as jnp
from jax import lax
from jax.sharding import PartitionSpec as P

EXPERTS = 4


def from_behind(value, axis, by):
    size = lax.axis_size(axis)
    pairs = [(i, i + by) for i in range(size) if 0 <= i + by < size]
    return lax.ppermute(value, axis, pairs)


def shards(in_flight, norm_gain, router_weight, up_weight, down_weight, chosen_experts):
    pipe_rank = lax.axis_index("pipe")
    last_rank = lax.axis_size("pipe") - 1
    devices = lax.axis_size("expert")
    group = lax.axis_index("expert") // (devices // EXPERTS)
    wide = in_flight[:, 0].astype(jnp.float32)
    legs, rows, width = wide.shape
    scale = lax.rsqrt(jnp.mean(wide * wide, axis=-1, keepdims=True) + 1e-06)
    normed = (wide * scale * norm_gain.astype(jnp.float32)).astype(jnp.bfloat16)
    affinity = jax.nn.sigmoid(
        jnp.einsum("lrd,lde->lre", normed, router_weight[:, 0], preferred_element_type=jnp.float32)
    )
    labels = jnp.arange(EXPERTS, dtype=jnp.int32)
    picked = jnp.sum(
        (chosen_experts[0, :, 0, :, :, None] == labels).astype(jnp.float32), axis=2
    )
    weighted = affinity * picked
    gates = weighted / jnp.sum(weighted, axis=-1, keepdims=True)
    gates = jnp.pad(gates, ((0, 0), (0, 0), (0, 128 - EXPERTS)))
    everyone = lax.all_gather(normed, "expert", axis=1, tiled=True)
    gates = lax.all_gather(gates, "expert", axis=1, tiled=True)
    gate = jnp.sum(jnp.where(jnp.arange(128) == group, gates, 0.0), axis=-1, keepdims=True)
    hidden = jnp.einsum(
        "lkd,ldh->lkh", everyone, up_weight[:, 0], preferred_element_type=jnp.float32
    )
    hidden = (jax.nn.silu(hidden) * gate).astype(jnp.bfloat16)
    partial = jnp.einsum(
        "lkh,lhd->lkd", hidden, down_weight[:, 0], preferred_element_type=jnp.float32
    ).astype(jnp.bfloat16)
    moe = lax.psum_scatter(partial, "expert", scatter_dimension=1, tiled=True)
    moved = (wide + moe.astype(jnp.float32)).astype(jnp.bfloat16)
    first_out, second_out = moved[0], moved[1]
    from_above = from_behind(first_out, "pipe", 1)
    from_below = from_behind(second_out, "pipe", -1)
    states = [
        jnp.where(pipe_rank == 0, second_out, from_above),
        jnp.where(pipe_rank == last_rank, first_out, from_below),
    ]
    return jnp.stack(states)[:, None]


def solution(mesh):
    in_specs = (
        P(None, "pipe", "expert", None),
        P(None, "pipe", None),
        P(None, "pipe", None, None),
        P(None, "pipe", None, "expert"),
        P(None, "pipe", "expert", None),
        P(None, None, "pipe", "expert", None),
    )
    out_specs = P(None, "pipe", "expert", None)
    return jax.shard_map(shards, mesh=mesh, in_specs=in_specs, out_specs=out_specs, check_vma=False)
```

time: 397 us -> 250 us (0.63)
  the two profiles are of different devices: /device:TPU:36 before, /device:TPU:88 now
where the time goes in v1:
time: 250 us
  waiting for transfers between devices  157 us (63%)
  blocking collectives  51.3 us (21%)
  between operations  13.5 us (5%)
  matrix products  13.2 us (5%)
  starting transfers between devices  7.59 us (3%)
  other arithmetic  6.75 us (3%)
    reduce_scatter x1, waiting for transfers between devices, shards(): moe = lax.psum_scatter(partial, 'expert', scatter_dimension=1, tiled=True)  122 us
    all_gather x1, blocking collectives, shards(): gates = lax.all_gather(gates, 'expert', axis=1, tiled=True)  51.3 us
    all_gather x1, waiting for transfers between devices, shards(): everyone = lax.all_gather(normed, 'expert', axis=1, tiled=True)  28.4 us
    dot_general x1, matrix products, shards(): jnp.einsum('lkh,lhd->lkd', hidden, down_weight[:, 0], preferred_element_t...  12 us
    ppermute x2, starting transfers between devices, from_behind(): return lax.ppermute(value, axis, pairs)  7.55 us
    ppermute x2, waiting for transfers between devices, from_behind(): return lax.ppermute(value, axis, pairs)  6.86 us
  transfers between devices with their start and end apart: 4, of which 4 were waited for; matrix products, arithmetic and copies ran while one was open for 1% of the time, Pallas kernels for 0%

profile of v1, /device:TPU:88, one launch (start us, length us, event | category | flops | bytes accessed | tf_op | source)
XLA Modules:
  0.0 250.0 jit_solution(12074518631736194984)
XLA Ops:
  6.5 0.0 copy-start
  6.5 0.0 all-gather.2.cloned.1.call-start
  6.5 0.9 bitcast_convert_fusion
  7.4 1.1 fusion.11
  8.5 1.8 fusion.13
  10.2 0.0 all-gather.2.cloned.1.call-update
  10.3 0.0 reduce-scatter.2.cloned.1.call-start
  10.3 0.7 convert_reduce_fusion
  11.0 1.2 fusion.19
  12.2 0.1 copy.23
  12.3 51.3 %all_gather.7 = f32[2,512,128]{2,0,1:T(2,128)S(1)} all-gather(f32[2,16,128]{2,0,1:T(2,128)S(1)} %pad.4.clone), channel_id=1, replica_groups=mesh['pipe'=16,'expert'=32] {'expert'}, dimensions={1}, use_global_device_ids=true | all-gather | bytes 540672 | tf_op jit(solution)/shard_map/all_gather | solution.py:35
  63.6 0.6 select_reduce_fusion
  64.3 0.1 copy.21
  64.4 28.4 %all-gather.2.cloned.1.call-done = bf16[2,512,3584]{2,1,0:T(8,128)(2,1)} async-done(((bf16[2,16,3584]{2,1,0:T(8,128)(2,1)}), bf16[2,512,3584]{2,1,0:T(8,128)(2,1)}) %all-gather.2.cloned.1.call-update) | async-done | bytes 7340048 | tf_op jit(solution)/shard_map/all_gather | solution.py:34
  92.8 0.0 copy-done
  92.8 12.0 %convolution_convert_fusion = bf16[2,512,3584]{2,1,0:T(8,128)(2,1)} fusion(bf16[2,1,128,3584]{3,2,1,0:T(8,128)(2,1)S(1)} %copy-done, bf16[2,512,3584]{2,1,0:T(8,128)(2,1)} %all-gather.2.cloned.1.call-done, bf16[2,1,3584,128]{3,2,1,0:T(8,128)(2,1)} %param.9, f32[2,512]{1,0:T(2,128)S(1)} %copy.21), kind=kOutput, calls=%fused_computation | convolution fusion | flops 1883504640 | bytes 18354176 | tf_op jit(solution)/shard_map/lkh,lhd->lkd/dot_general | solution.py:41
  104.8 0.0 copy-start.1
  104.8 0.0 reduce-scatter.2.cloned.1.call-update
  104.9 122.2 %reduce-scatter.2.cloned.1.call-done = bf16[2,16,3584]{2,1,0:T(8,128)(2,1)} async-done(((bf16[2,512,3584]{2,1,0:T(8,128)(2,1)}), bf16[2,16,3584]{2,1,0:T(8,128)(2,1)}) %reduce-scatter.2.cloned.1.call-update) | async-done | bytes 229392 | tf_op jit(solution)/shard_map/reduce_scatter | solution.py:44
  227.0 0.0 copy-done.1
  227.0 1.0 fusion.14
  228.0 5.6 %collective-permute-start = (bf16[16,3584]{1,0:T(8,128)(2,1)S(1)}, bf16[16,3584]{1,0:T(8,128)(2,1)S(1)}, u32[]{:S(2)}, u32[]{:S(2)}) collective-permute-start(bf16[16,3584]{1,0:T(8,128)(2,1)S(1)} %get-tuple-element.7), channel_id=1, source_target_pairs={{0,32},{32,64},{64,96},{96,128},{128,160},{160,192},{192,224},{224... | collective-permute-start | bytes 344072 | tf_op jit(solution)/shard_map/ppermute | solution.py:12
  233.7 1.9 collective-permute-start.1
  235.6 0.4 collective-permute-done
  236.0 6.4 %collective-permute-done.1 = bf16[16,3584]{1,0:T(8,128)(2,1)S(1)} collective-permute-done((bf16[16,3584]{1,0:T(8,128)(2,1)S(1)}, bf16[16,3584]{1,0:T(8,128)(2,1)S(1)}, u32[]{:S(2)}, u32[]{:S(2)}) %collective-permute-start.1) | collective-permute-done | bytes 114720 | tf_op jit(solution)/shard_map/ppermute | solution.py:12
  242.5 0.7 maximum_bitcast_fusion
  (6 shorter events, 0.1 us)
Async XLA Ops:
  6.5 86.3 %copy-start = (bf16[2,1,128,3584]{3,2,1,0:T(8,128)(2,1)S(1)}, bf16[2,1,128,3584]{3,2,1,0:T(8,128)(2,1)}, u32[]{:S(2)}) copy-start(bf16[2,1,128,3584]{3,2,1,0:T(8,128)(2,1)} %param.10) | copy-start | bytes 5505028
  6.5 86.3 %all-gather.2.cloned.1.call-start = ((), (), s32[]{:S(2)}) async-start(), calls=%async_computation.1 | async-start | bytes 7569408 | tf_op jit(solution)/shard_map/all_gather | solution.py:34
  10.3 216.7 %reduce-scatter.2.cloned.1.call-start = ((), (), s32[]{:S(2)}) async-start(), calls=%async_computation.2 | async-start | bytes 7569408 | tf_op jit(solution)/shard_map/reduce_scatter | solution.py:44
  104.8 122.2 %copy-start.1 = (bf16[2,1,16,3584]{3,2,1,0:T(8,128)(2,1)S(1)}, bf16[2,1,16,3584]{3,2,1,0:T(8,128)(2,1)}, u32[]{:S(2)}) copy-start(bf16[2,1,16,3584]{3,2,1,0:T(8,128)(2,1)} %param.6) | copy-start | bytes 688132
  228.0 8.0 %collective-permute-start = (bf16[16,3584]{1,0:T(8,128)(2,1)S(1)}, bf16[16,3584]{1,0:T(8,128)(2,1)S(1)}, u32[]{:S(2)}, u32[]{:S(2)}) collective-permute-start(bf16[16,3584]{1,0:T(8,128)(2,1)S(1)} %get-tuple-element.7), channel_id=1, source_target_pairs={{0,32},{32,64},{64,96},{96,128},{128,160},{160,192},{192,224},{224... | collective-permute-start | bytes 344072 | tf_op jit(solution)/shard_map/ppermute | solution.py:12
  233.7 8.8 %collective-permute-start.1 = (bf16[16,3584]{1,0:T(8,128)(2,1)S(1)}, bf16[16,3584]{1,0:T(8,128)(2,1)S(1)}, u32[]{:S(2)}, u32[]{:S(2)}) collective-permute-start(bf16[16,3584]{1,0:T(8,128)(2,1)S(1)} %get-tuple-element.8), channel_id=1, source_target_pairs={{32,0},{64,32},{96,64},{128,96},{160,128},{192,160},{224,192},{256... | collective-permute-start | bytes 344072 | tf_op jit(solution)/shard_map/ppermute | solution.py:12
Sparse Core Ops, SparseCore 0:
  10.5 82.2 all-gather.1
  105.0 121.9 reduce-scatter.1

commit v2 on v1

v2 whole, which is shorter than its diff:
```python
import jax
import jax.numpy as jnp
from jax import lax
from jax.experimental import pallas as pl
from jax.experimental.pallas import tpu as pltpu
from jax.sharding import PartitionSpec as P

EXPERTS = 4
RING = 4
CORES = 2
LEGS = 2
LANES = 128
TILE = 512
ORDER = (2, 1, 3, 0)


def from_behind(value, axis, by):
    size = lax.axis_size(axis)
    pairs = [(i, i + by) for i in range(size) if 0 <= i + by < size]
    return lax.ppermute(value, axis, pairs)


def kernel(own, wide, up_hbm, down_hbm, out, rows_in, part, near, early, late, zearly, zlate,
           up, down, send, recv, local):
    width = out.shape[-1]
    me = lax.axis_index("expert")
    z, x, c = me // (RING * CORES), (me // CORES) % RING, me % CORES

    def at(zz, xx, cc):
        return (zz * RING + xx) * CORES + cc

    def turn(v, by):
        return (v + by) % RING

    zp, zm = at(turn(z, 1), x, c), at(turn(z, 3), x, c)
    xp, xm = at(z, turn(x, 1), c), at(z, turn(x, 3), c)
    sib = at(z, x, 1 - c)

    weights = [
        pltpu.make_async_copy(up_hbm, up, local.at[0]),
        pltpu.make_async_copy(down_hbm, down, local.at[1]),
    ]
    for copy in weights:
        copy.start()

    barrier = pltpu.get_barrier_semaphore()
    for device in (zp, zm, xp, xm, sib):
        pl.semaphore_signal(
            barrier, inc=1, device_id={"expert": device}, device_id_type=pl.DeviceIdType.MESH
        )
    pl.semaphore_wait(barrier, 5)

    started = {}

    def go(name, src, dst, device):
        number = len(started)
        copy = pltpu.make_async_remote_copy(
            src_ref=src,
            dst_ref=dst,
            send_sem=send.at[number],
            recv_sem=recv.at[number],
            device_id={"expert": device},
            device_id_type=pl.DeviceIdType.MESH,
        )
        copy.start()
        started[name] = copy

    def got(*name):
        started[name].wait_recv()

    def slot(dx, dz):
        return rows_in.at[turn(x, dx), c, turn(z, dz)]

    def spread(dz):
        src = own if dz == 0 else slot(0, dz)
        go(("x1p", dz), src, slot(0, dz), xp)
        go(("x1m", dz), src, slot(0, dz), xm)
        go(("c", 0, dz), src, slot(0, dz), sib)

    def relay(dz):
        got("x1p", dz)
        go(("x2p", dz), slot(3, dz).at[0], slot(3, dz).at[0], xp)
        go(("c", 3, dz), slot(3, dz), slot(3, dz), sib)
        got("x1m", dz)
        go(("x2m", dz), slot(1, dz).at[1], slot(1, dz).at[1], xm)
        go(("c", 1, dz), slot(1, dz), slot(1, dz), sib)

    def finish(dz):
        got("x2p", dz)
        go(("c2p", dz), slot(2, dz).at[0], slot(2, dz).at[0], sib)
        got("x2m", dz)
        go(("c2m", dz), slot(2, dz).at[1], slot(2, dz).at[1], sib)

    def compute(dx):
        xx = turn(x, dx)

        def leg_body(leg, carry):
            lhs = rows_in[xx, :, :, leg]
            flat = lhs.reshape(CORES * RING * lhs.shape[2], lhs.shape[3])
            lane = lax.broadcasted_iota(jnp.int32, (1, LANES), 1)
            mine = (lane == z) | (lane == z + EXPERTS)
            gate = jnp.sum(
                jnp.where(mine, flat[:, width:].astype(jnp.float32), 0.0), axis=1, keepdims=True
            )
            hidden = jnp.dot(flat[:, :width], up[leg], preferred_element_type=jnp.float32)
            hidden = (hidden / (1.0 + jnp.exp(-hidden)) * gate).astype(jnp.bfloat16)

            def tile_body(tile, carry):
                columns = pl.ds(pl.multiple_of(tile * TILE, TILE), TILE)
                value = jnp.dot(hidden, down[leg, :, columns], preferred_element_type=jnp.float32)
                part[xx, :, :, leg, :, columns] = value.astype(jnp.bfloat16).reshape(
                    CORES, RING, lhs.shape[2], TILE
                )
                return carry

            return lax.fori_loop(0, width // TILE, tile_body, carry)

        lax.fori_loop(0, LEGS, leg_body, 0)
        go(("near", dx), part.at[xx, 1 - c], near.at[dx], sib)

    def pair(dx):
        got("near", dx)
        xx = turn(x, dx)

        def body(zz, carry):
            total = part[xx, c, zz].astype(jnp.float32) + near[dx, zz].astype(jnp.float32)
            part[xx, c, zz] = total.astype(jnp.bfloat16)
            return carry

        lax.fori_loop(0, RING, body, 0)

    def mine(dx, dz, leg):
        return part.at[turn(x, dx), c, turn(z, dz), leg]

    def add(ref, other):
        ref[...] = (ref[...].astype(jnp.float32) + other[...].astype(jnp.float32)).astype(
            jnp.bfloat16
        )

    go(("z1p",), own, slot(0, 0), zp)
    go(("z1m",), own, slot(0, 0), zm)
    spread(0)
    rows_in[x, c, z] = own[...]
    got("z1p")
    go(("z2p",), slot(0, 3).at[0], slot(0, 3).at[0], zp)
    spread(3)
    got("z1m")
    go(("z2m",), slot(0, 1).at[1], slot(0, 1).at[1], zm)
    spread(1)
    relay(0)
    got("z2p")
    got("z2m")
    spread(2)
    for copy in weights:
        copy.wait()
    relay(3)
    relay(1)
    for dz in (0, 3, 1, 2):
        got("c", 0, dz)
    compute(0)
    relay(2)
    for dz in (0, 3, 1, 2):
        got("c", 3, dz)
    for dz in (0, 3, 1, 2):
        got("c", 1, dz)
    finish(0)
    compute(1)
    finish(3)
    compute(3)
    pair(1)
    for dz in ORDER:
        go(("late", 1, dz), mine(1, dz, 1), late.at[0, turn(z, dz), 1], xp)
    pair(3)
    for dz in ORDER:
        go(("late", 0, dz), mine(3, dz, 0), late.at[1, turn(z, dz), 0], xm)
    finish(1)
    finish(2)
    for dz in (0, 3, 1, 2):
        got("c2p", dz)
        got("c2m", dz)
    compute(2)
    pair(0)
    pair(2)
    for dz in ORDER:
        go(("early", 0, dz), mine(2, dz, 0), early.at[0, turn(z, dz)], xp)
        go(("early", 1, dz), mine(2, dz, 1), early.at[1, turn(z, dz)], xm)
    for dz in ORDER:
        got("early", 0, dz)
        add(mine(1, dz, 0), early.at[0, turn(z, dz)])
        go(("late", 2, dz), mine(1, dz, 0), late.at[0, turn(z, dz), 0], xp)
        got("early", 1, dz)
        add(mine(3, dz, 1), early.at[1, turn(z, dz)])
        go(("late", 3, dz), mine(3, dz, 1), late.at[1, turn(z, dz), 1], xm)

    def settle(dz):
        for number in range(4):
            got("late", number, dz)
        zz = turn(z, dz)
        total = part[x, c, zz].astype(jnp.float32) + late[0, zz].astype(jnp.float32)
        part[x, c, zz] = (total + late[1, zz].astype(jnp.float32)).astype(jnp.bfloat16)

    settle(2)
    go(("zearly", 0), mine(0, 2, 0), zearly.at[0], zp)
    go(("zearly", 1), mine(0, 2, 1), zearly.at[1], zm)
    settle(1)
    go(("zlate", 0), mine(0, 1, 1), zlate.at[0, 1], zp)
    settle(3)
    go(("zlate", 1), mine(0, 3, 0), zlate.at[1, 0], zm)
    got("zearly", 0)
    add(mine(0, 1, 0), zearly.at[0])
    go(("zlate", 2), mine(0, 1, 0), zlate.at[0, 0], zp)
    got("zearly", 1)
    add(mine(0, 3, 1), zearly.at[1])
    go(("zlate", 3), mine(0, 3, 1), zlate.at[1, 1], zm)
    settle(0)
    for number in range(4):
        got("zlate", number)
    total = wide[...].astype(jnp.float32) + part[x, c, z].astype(jnp.float32)
    total = total + zlate[0].astype(jnp.float32) + zlate[1].astype(jnp.float32)
    out[...] = total.astype(out.dtype)
    for copy in started.values():
        copy.wait_send()


def experts(packed, tokens, up, down):
    legs, rows, wide = packed.shape
    width = tokens.shape[2]
    vmem = pl.BlockSpec(memory_space=pltpu.VMEM)
    anywhere = pl.BlockSpec(memory_space=pl.ANY)
    copies = 88
    return pl.pallas_call(
        kernel,
        out_shape=jax.ShapeDtypeStruct(tokens.shape, jnp.bfloat16),
        in_specs=[vmem, vmem, anywhere, anywhere],
        out_specs=vmem,
        scratch_shapes=[
            pltpu.VMEM((RING, CORES, RING, legs, rows, wide), jnp.bfloat16),
            pltpu.VMEM((RING, CORES, RING, legs, rows, width), jnp.bfloat16),
            pltpu.VMEM((RING, RING, legs, rows, width), jnp.bfloat16),
            pltpu.VMEM((2, RING, rows, width), jnp.bfloat16),
            pltpu.VMEM((2, RING, legs, rows, width), jnp.bfloat16),
            pltpu.VMEM((2, rows, width), jnp.bfloat16),
            pltpu.VMEM((2, legs, rows, width), jnp.bfloat16),
            pltpu.VMEM(up.shape, up.dtype),
            pltpu.VMEM(down.shape, down.dtype),
            pltpu.SemaphoreType.DMA((copies,)),
            pltpu.SemaphoreType.DMA((copies,)),
            pltpu.SemaphoreType.DMA((2,)),
        ],
        compiler_params=pltpu.CompilerParams(
            collective_id=0, has_side_effects=True, vmem_limit_bytes=48 * 1024 * 1024
        ),
        name="experts",
    )(packed, tokens, up, down)


def shards(in_flight, norm_gain, router_weight, up_weight, down_weight, chosen_experts):
    pipe_rank = lax.axis_index("pipe")
    last_rank = lax.axis_size("pipe") - 1
    tokens = in_flight[:, 0]
    wide = tokens.astype(jnp.float32)
    scale = lax.rsqrt(jnp.mean(wide * wide, axis=-1, keepdims=True) + 1e-06)
    normed = (wide * scale * norm_gain.astype(jnp.float32)).astype(jnp.bfloat16)
    affinity = jax.nn.sigmoid(
        jnp.einsum("lrd,lde->lre", normed, router_weight[:, 0], preferred_element_type=jnp.float32)
    )
    labels = jnp.arange(EXPERTS, dtype=jnp.int32)
    picked = jnp.sum(
        (chosen_experts[0, :, 0, :, :, None] == labels).astype(jnp.float32), axis=2
    )
    weighted = affinity * picked
    gates = weighted / jnp.sum(weighted, axis=-1, keepdims=True)
    high = gates.astype(jnp.bfloat16)
    low = (gates - high.astype(jnp.float32)).astype(jnp.bfloat16)
    empty = jnp.zeros(gates.shape[:2] + (LANES - 2 * EXPERTS,), jnp.bfloat16)
    packed = jnp.concatenate([normed, high, low, empty], axis=-1)
    moved = experts(packed, tokens, up_weight[:, 0], down_weight[:, 0])
    first_out, second_out = moved[0], moved[1]
    from_above = from_behind(first_out, "pipe", 1)
    from_below = from_behind(second_out, "pipe", -1)
    states = [
        jnp.where(pipe_rank == 0, second_out, from_above),
        jnp.where(pipe_rank == last_rank, first_out, from_below),
    ]
    return jnp.stack(states)[:, None]


def solution(mesh):
    in_specs = (
        P(None, "pipe", "expert", None),
        P(None, "pipe", None),
        P(None, "pipe", None, None),
        P(None, "pipe", None, "expert"),
        P(None, "pipe", "expert", None),
        P(None, None, "pipe", "expert", None),
    )
    out_specs = P(None, "pipe", "expert", None)
    return jax.shard_map(shards, mesh=mesh, in_specs=in_specs, out_specs=out_specs, check_vma=False)
```

time: 250 us -> 112 us (0.45)
  the two profiles are of different devices: /device:TPU:88 before, /device:TPU:94 now
where the time goes in v2:
time: 112 us; the launch traced here: 111 us
  Pallas kernels  91.3 us (82%)
  waiting for transfers between devices  6.05 us (5%)
  starting transfers between devices  5.84 us (5%)
  other arithmetic  4.38 us (4%)
  local copies, waits for them, and re-layouts  3.21 us (3%)
    pallas_call x1, Pallas kernels, experts(): pl.pallas_call(kernel, out_shape=jax.ShapeDtypeStruct(tokens.shape, jnp.b...  91.3 us
    ppermute x2, waiting for transfers between devices, from_behind(): return lax.ppermute(value, axis, pairs)  6.05 us
    ppermute x2, starting transfers between devices, from_behind(): return lax.ppermute(value, axis, pairs)  5.84 us
    unnamed x8, local copies, waits for them, and re-layouts  3 us
  transfers between devices with their start and end apart: 2, of which 2 were waited for; matrix products, arithmetic and copies ran while one was open for 0% of the time, Pallas kernels for 0%

profile of v2, /device:TPU:94, one launch (start us, length us, event | category | flops | bytes accessed | tf_op | source)
XLA Modules:
  0.0 111.2 jit_solution(13464255686690881249)
XLA Ops:
  0.0 0.0 copy-start
  0.0 0.0 copy-start.1
  0.0 1.1 %fusion.6 = f32[2,16]{1,0:T(2,128)S(1)} fusion(bf16[2,1,16,3584]{3,2,1,0:T(8,128)(2,1)} %param.6), kind=kLoop, calls=%fused_computation.9 | loop fusion | flops 344032 | bytes 229504 | tf_op jit(solution)/shard_map/reduce_sum | solution.py:262
  1.2 0.7 convert_reduce_fusion
  1.9 0.1 copy.16
  2.0 0.7 bitcast_convert_fusion
  2.7 1.1 fusion.8
  3.8 0.0 copy-done
  3.8 0.3 subtract_convert_fusion
  4.1 0.1 concatenate.3.own
  4.2 0.0 copy-done.1
  4.2 0.0 copy-start.2
  4.2 1.5 %copy-done.2 = bf16[2,1,3584,128]{3,2,1,0:T(8,128)(2,1)S(1)} copy-done((bf16[2,1,3584,128]{3,2,1,0:T(8,128)(2,1)S(1)}, bf16[2,1,3584,128]{3,2,1,0:T(8,128)(2,1)}, u32[]{:S(2)}) %copy-start.2) | copy-done | bytes 1835032
  5.7 0.0 copy-start.3
  5.7 1.5 %copy-done.3 = bf16[2,1,128,3584]{3,2,1,0:T(8,128)(2,1)S(1)} copy-done((bf16[2,1,128,3584]{3,2,1,0:T(8,128)(2,1)S(1)}, bf16[2,1,128,3584]{3,2,1,0:T(8,128)(2,1)}, u32[]{:S(2)}) %copy-start.3) | copy-done | bytes 1835032
  7.2 91.3 %experts.1 = bf16[2,16,3584]{2,1,0:T(8,128)(2,1)S(1)} custom-call(bf16[2,16,3712]{2,1,0:T(8,128)(2,1)S(1)} %concatenate.3.own, bf16[2,16,3584]{2,1,0:T(8,128)(2,1)S(1)} %bitcast.31, bf16[2,3584,128]{2,1,0:T(8,128)(2,1)S(1)} %bitcast.32, bf16[2,128,3584]{2,1,0:T(8,128)(2,1)S(1)} %bitcast.33), custom_call_target="tpu_custom_call" | custom-call | tf_op jit(solution)/shard_map/experts/pallas_call | solution.py:231
  98.6 3.1 %collective-permute-start = (bf16[16,3584]{1,0:T(8,128)(2,1)S(1)}, bf16[16,3584]{1,0:T(8,128)(2,1)S(1)}, u32[]{:S(2)}, u32[]{:S(2)}) collective-permute-start(bf16[16,3584]{1,0:T(8,128)(2,1)S(1)} %get-tuple-element.9), channel_id=1, source_target_pairs={{0,32},{32,64},{64,96},{96,128},{128,160},{160,192},{192,224},{224... | collective-permute-start | bytes 344072 | tf_op jit(solution)/shard_map/ppermute | solution.py:20
  101.7 2.7 %collective-permute-start.1 = (bf16[16,3584]{1,0:T(8,128)(2,1)S(1)}, bf16[16,3584]{1,0:T(8,128)(2,1)S(1)}, u32[]{:S(2)}, u32[]{:S(2)}) collective-permute-start(bf16[16,3584]{1,0:T(8,128)(2,1)S(1)} %get-tuple-element.10), channel_id=1, source_target_pairs={{32,0},{64,32},{96,64},{128,96},{160,128},{192,160},{224,192},{256... | collective-permute-start | bytes 344072 | tf_op jit(solution)/shard_map/ppermute | solution.py:20
  104.4 0.8 collective-permute-done
  105.2 5.2 %collective-permute-done.1 = bf16[16,3584]{1,0:T(8,128)(2,1)S(1)} collective-permute-done((bf16[16,3584]{1,0:T(8,128)(2,1)S(1)}, bf16[16,3584]{1,0:T(8,128)(2,1)S(1)}, u32[]{:S(2)}, u32[]{:S(2)}) %collective-permute-start.1) | collective-permute-done | bytes 114720 | tf_op jit(solution)/shard_map/ppermute | solution.py:20
  110.5 0.7 maximum_bitcast_fusion
  (4 shorter events, 0.1 us)
Async XLA Ops:
  0.0 3.8 %copy-start = (bf16[2,1,3584,4]{2,3,1,0:T(4,128)(2,1)S(1)}, bf16[2,1,3584,4]{2,3,1,0:T(4,128)(2,1)}, u32[]{:S(2)}) copy-start(bf16[2,1,3584,4]{2,3,1,0:T(4,128)(2,1)} %param.8) | copy-start | bytes 172036
  0.0 4.2 %copy-start.1 = (bf16[2,1,16,3584]{3,2,1,0:T(8,128)(2,1)S(1)}, bf16[2,1,16,3584]{3,2,1,0:T(8,128)(2,1)}, u32[]{:S(2)}) copy-start(bf16[2,1,16,3584]{3,2,1,0:T(8,128)(2,1)} %param.6) | copy-start | bytes 688132
  4.2 1.5 %copy-start.2 = (bf16[2,1,3584,128]{3,2,1,0:T(8,128)(2,1)S(1)}, bf16[2,1,3584,128]{3,2,1,0:T(8,128)(2,1)}, u32[]{:S(2)}) copy-start(bf16[2,1,3584,128]{3,2,1,0:T(8,128)(2,1)} %param.9) | copy-start | bytes 5505028
  5.7 1.5 %copy-start.3 = (bf16[2,1,128,3584]{3,2,1,0:T(8,128)(2,1)S(1)}, bf16[2,1,128,3584]{3,2,1,0:T(8,128)(2,1)}, u32[]{:S(2)}) copy-start(bf16[2,1,128,3584]{3,2,1,0:T(8,128)(2,1)} %param.10) | copy-start | bytes 5505028
  98.6 6.7 %collective-permute-start = (bf16[16,3584]{1,0:T(8,128)(2,1)S(1)}, bf16[16,3584]{1,0:T(8,128)(2,1)S(1)}, u32[]{:S(2)}, u32[]{:S(2)}) collective-permute-start(bf16[16,3584]{1,0:T(8,128)(2,1)S(1)} %get-tuple-element.9), channel_id=1, source_target_pairs={{0,32},{32,64},{64,96},{96,128},{128,160},{160,192},{192,224},{224... | collective-permute-start | bytes 344072 | tf_op jit(solution)/shard_map/ppermute | solution.py:20
  101.7 8.8 %collective-permute-start.1 = (bf16[16,3584]{1,0:T(8,128)(2,1)S(1)}, bf16[16,3584]{1,0:T(8,128)(2,1)S(1)}, u32[]{:S(2)}, u32[]{:S(2)}) collective-permute-start(bf16[16,3584]{1,0:T(8,128)(2,1)S(1)} %get-tuple-element.10), channel_id=1, source_target_pairs={{32,0},{64,32},{96,64},{128,96},{160,128},{192,160},{224,192},{256... | collective-permute-start | bytes 344072 | tf_op jit(solution)/shard_map/ppermute | solution.py:20

commit v3 on v2

--- a/solution.py
+++ b/solution.py
@@ -14,14 +14,9 @@
 ORDER = (2, 1, 3, 0)
 
 
-def from_behind(value, axis, by):
-    size = lax.axis_size(axis)
-    pairs = [(i, i + by) for i in range(size) if 0 <= i + by < size]
-    return lax.ppermute(value, axis, pairs)
-
-
 def kernel(own, wide, up_hbm, down_hbm, out, rows_in, part, near, early, late, zearly, zlate,
-           up, down, send, recv, local):
+           moved, arrived, up, down, send, recv, local,
+           pipe_send, pipe_recv):
     width = out.shape[-1]
     me = lax.axis_index("expert")
     z, x, c = me // (RING * CORES), (me // CORES) % RING, me % CORES
@@ -48,7 +43,13 @@
         pl.semaphore_signal(
             barrier, inc=1, device_id={"expert": device}, device_id_type=pl.DeviceIdType.MESH
         )
-    pl.semaphore_wait(barrier, 5)
+    rank, ranks = lax.axis_index("pipe"), lax.axis_size("pipe")
+    above, below = (rank + 1) % ranks, (rank + ranks - 1) % ranks
+    for device in (above, below):
+        pl.semaphore_signal(
+            barrier, inc=1, device_id={"pipe": device}, device_id_type=pl.DeviceIdType.MESH
+        )
+    pl.semaphore_wait(barrier, 7)
 
     started = {}
 
@@ -181,10 +182,11 @@
     compute(2)
     pair(0)
     pair(2)
-    for dz in ORDER:
+    def depart(dz):
         go(("early", 0, dz), mine(2, dz, 0), early.at[0, turn(z, dz)], xp)
         go(("early", 1, dz), mine(2, dz, 1), early.at[1, turn(z, dz)], xm)
-    for dz in ORDER:
+
+    def onward(dz):
         got("early", 0, dz)
         add(mine(1, dz, 0), early.at[0, turn(z, dz)])
         go(("late", 2, dz), mine(1, dz, 0), late.at[0, turn(z, dz), 0], xp)
@@ -199,9 +201,17 @@
         total = part[x, c, zz].astype(jnp.float32) + late[0, zz].astype(jnp.float32)
         part[x, c, zz] = (total + late[1, zz].astype(jnp.float32)).astype(jnp.bfloat16)
 
+    depart(2)
+    depart(1)
+    depart(3)
+    onward(2)
+    depart(0)
+    onward(1)
+    onward(3)
     settle(2)
     go(("zearly", 0), mine(0, 2, 0), zearly.at[0], zp)
     go(("zearly", 1), mine(0, 2, 1), zearly.at[1], zm)
+    onward(0)
     settle(1)
     go(("zlate", 0), mine(0, 1, 1), zlate.at[0, 1], zp)
     settle(3)
@@ -213,11 +223,54 @@
     add(mine(0, 3, 1), zearly.at[1])
     go(("zlate", 3), mine(0, 3, 1), zlate.at[1, 1], zm)
     settle(0)
-    for number in range(4):
-        got("zlate", number)
-    total = wide[...].astype(jnp.float32) + part[x, c, z].astype(jnp.float32)
-    total = total + zlate[0].astype(jnp.float32) + zlate[1].astype(jnp.float32)
-    out[...] = total.astype(out.dtype)
+    last = ranks - 1
+
+    def hand(leg, device):
+        return pltpu.make_async_remote_copy(
+            src_ref=moved.at[leg],
+            dst_ref=arrived.at[leg],
+            send_sem=pipe_send.at[leg],
+            recv_sem=pipe_recv.at[leg],
+            device_id={"pipe": device},
+            device_id_type=pl.DeviceIdType.MESH,
+        )
+
+    first, second = hand(0, above), hand(1, below)
+
+    def total(leg):
+        value = wide[leg].astype(jnp.float32) + part[x, c, z, leg].astype(jnp.float32)
+        value = value + zlate[0, leg].astype(jnp.float32) + zlate[1, leg].astype(jnp.float32)
+        moved[leg] = value.astype(jnp.bfloat16)
+
+    got("zlate", 1)
+    got("zlate", 2)
+    total(0)
+    pl.when(rank < last)(first.start)
+    got("zlate", 0)
+    got("zlate", 3)
+    total(1)
+    pl.when(rank > 0)(second.start)
+
+    @pl.when(rank == 0)
+    def _():
+        out[0] = moved[1]
+
+    @pl.when(rank == last)
+    def _():
+        out[1] = moved[0]
+
+    @pl.when(rank > 0)
+    def _():
+        first.wait_recv()
+        out[0] = arrived[0]
+
+    @pl.when(rank < last)
+    def _():
+        second.wait_recv()
+        out[1] = arrived[1]
+
+    pl.when(rank < last)(first.wait_send)
+    pl.when(rank > 0)(second.wait_send)
     for copy in started.values():
         copy.wait_send()
 
@@ -241,22 +294,24 @@
             pltpu.VMEM((2, RING, legs, rows, width), jnp.bfloat16),
             pltpu.VMEM((2, rows, width), jnp.bfloat16),
             pltpu.VMEM((2, legs, rows, width), jnp.bfloat16),
+            pltpu.VMEM(tokens.shape, jnp.bfloat16),
+            pltpu.VMEM(tokens.shape, jnp.bfloat16),
             pltpu.VMEM(up.shape, up.dtype),
             pltpu.VMEM(down.shape, down.dtype),
             pltpu.SemaphoreType.DMA((copies,)),
             pltpu.SemaphoreType.DMA((copies,)),
             pltpu.SemaphoreType.DMA((2,)),
+            pltpu.SemaphoreType.DMA((2,)),
+            pltpu.SemaphoreType.DMA((2,)),
         ],
         compiler_params=pltpu.CompilerParams(
-            collective_id=0, has_side_effects=True, vmem_limit_bytes=48 * 1024 * 1024
+            collective_id=0, has_side_effects=True, vmem_limit_bytes=66000000
         ),
         name="experts",
     )(packed, tokens, up, down)
 
 
 def shards(in_flight, norm_gain, router_weight, up_weight, down_weight, chosen_experts):
-    pipe_rank = lax.axis_index("pipe")
-    last_rank = lax.axis_size("pipe") - 1
     tokens = in_flight[:, 0]
     wide = tokens.astype(jnp.float32)
     scale = lax.rsqrt(jnp.mean(wide * wide, axis=-1, keepdims=True) + 1e-06)
@@ -274,15 +329,7 @@
     low = (gates - high.astype(jnp.float32)).astype(jnp.bfloat16)
     empty = jnp.zeros(gates.shape[:2] + (LANES - 2 * EXPERTS,), jnp.bfloat16)
     packed = jnp.concatenate([normed, high, low, empty], axis=-1)
-    moved = experts(packed, tokens, up_weight[:, 0], down_weight[:, 0])
-    first_out, second_out = moved[0], moved[1]
-    from_above = from_behind(first_out, "pipe", 1)
-    from_below = from_behind(second_out, "pipe", -1)
-    states = [
-        jnp.where(pipe_rank == 0, second_out, from_above),
-        jnp.where(pipe_rank == last_rank, first_out, from_below),
-    ]
-    return jnp.stack(states)[:, None]
+    return experts(packed, tokens, up_weight[:, 0], down_weight[:, 0])[:, None]
 
 
 def solution(mesh):

time: 112 us -> 109 us (0.973)
  the two profiles are of different devices: /device:TPU:94 before, /device:TPU:64 now
where the time goes in v3:
time: 109 us; the launch traced here: 108 us
  Pallas kernels  102 us (94%)
  other arithmetic  3.58 us (3%)
  local copies, waits for them, and re-layouts  2.51 us (2%)
    pallas_call x1, Pallas kernels, experts(): pl.pallas_call(kernel, out_shape=jax.ShapeDtypeStruct(tokens.shape, jnp.b...  102 us

profile of v3, /device:TPU:64, one launch (start us, length us, event | category | flops | bytes accessed | tf_op | source)
XLA Modules:
  0.0 108.4 jit_solution(9905084020961113426)
XLA Ops:
  0.0 0.0 copy-start
  0.0 1.1 fusion.6
  1.1 0.7 convert_reduce_fusion
  1.8 0.1 copy.16
  1.9 0.7 bitcast_convert_fusion
  2.6 1.1 fusion.8
  3.7 0.0 copy-done
  3.7 0.3 subtract_convert_fusion
  4.0 0.8 concatenate.3.own
  4.8 102.0 %experts.1 = bf16[2,16,3584]{2,1,0:T(8,128)(2,1)} custom-call(bf16[2,16,3712]{2,1,0:T(8,128)(2,1)} %concatenate.3.own, bf16[2,16,3584]{2,1,0:T(8,128)(2,1)} %bitcast.18, bf16[2,3584,128]{2,1,0:T(8,128)(2,1)} %bitcast.19, bf16[2,128,3584]{2,1,0:T(8,128)(2,1)} %bitcast.20), custom_call_target="tpu_custom_call" | custom-call | tf_op jit(solution)/shard_map/experts/pallas_call | solution.py:284
  106.8 1.6 %copy.20 = bf16[2,1,16,3584]{3,2,1,0:T(8,128)(2,1)} copy(bf16[2,1,16,3584]{3,2,1,0:T(8,128)(2,1)} %bitcast.21) | data formatting | bytes 458752
  (2 shorter events, 0.0 us)
Async XLA Ops:
  0.0 3.7 %copy-start = (bf16[2,1,3584,4]{2,3,1,0:T(4,128)(2,1)S(1)}, bf16[2,1,3584,4]{2,3,1,0:T(4,128)(2,1)}, u32[]{:S(2)}) copy-start(bf16[2,1,3584,4]{2,3,1,0:T(4,128)(2,1)} %param.8) | copy-start | bytes 172036

commit v4 on v3

--- a/solution.py
+++ b/solution.py
@@ -14,8 +14,8 @@
 ORDER = (2, 1, 3, 0)
 
 
-def kernel(own, wide, up_hbm, down_hbm, out, rows_in, part, near, early, late, zearly, zlate,
-           moved, arrived, up, down, send, recv, local,
+def kernel(wide, gain, router, chosen, up_hbm, down_hbm, moved, out, own, rows_in, part, near, early, late, zearly, zlate,
+           arrived, up, down, send, recv, local,
            pipe_send, pipe_recv):
     width = out.shape[-1]
     me = lax.axis_index("expert")
@@ -49,6 +49,28 @@
         pl.semaphore_signal(
             barrier, inc=1, device_id={"pipe": device}, device_id_type=pl.DeviceIdType.MESH
         )
+
+    lane = lax.broadcasted_iota(jnp.int32, (1, LANES), 1)
+    label = lane % EXPERTS
+    for leg in range(LEGS):
+        value = wide[leg].astype(jnp.float32)
+        scale = lax.rsqrt(jnp.mean(value * value, axis=-1, keepdims=True) + 1e-06)
+        normed = (value * scale * gain[...].astype(jnp.float32)[leg : leg + 1]).astype(jnp.bfloat16)
+        own[leg, :, :width] = normed
+        normed = normed.astype(jnp.float32)
+        logits = jnp.zeros((normed.shape[0], LANES), jnp.float32)
+        for expert in range(EXPERTS):
+            column = router[leg, expert : expert + 1].astype(jnp.float32)
+            logit = jnp.sum(normed * column, axis=-1, keepdims=True)
+            logits = jnp.where(label == expert, logit, logits)
+        named = (chosen[leg, :, 0:1] == label) | (chosen[leg, :, 1:2] == label)
+        weighted = jnp.where(named, jax.nn.sigmoid(logits), 0.0)
+        first_four = jnp.where(lane < EXPERTS, weighted, 0.0)
+        gates = weighted / jnp.sum(first_four, axis=-1, keepdims=True)
+        high = gates.astype(jnp.bfloat16).astype(jnp.float32)
+        gates = jnp.where(lane < EXPERTS, high, jnp.where(lane < 2 * EXPERTS, gates - high, 0.0))
+        own[leg, :, width:] = gates.astype(jnp.bfloat16)
+
     pl.semaphore_wait(barrier, 7)
 
     started = {}
@@ -253,11 +275,11 @@
 
     @pl.when(rank == 0)
     def _():
-        out[0] = moved[1]
+        out[0] = jnp.zeros(out.shape[1:], out.dtype)
 
     @pl.when(rank == last)
     def _():
-        out[1] = moved[0]
+        out[1] = jnp.zeros(out.shape[1:], out.dtype)
 
     @pl.when(rank > 0)
     def _():
@@ -275,18 +297,19 @@
         copy.wait_send()
 
 
-def experts(packed, tokens, up, down):
-    legs, rows, wide = packed.shape
-    width = tokens.shape[2]
+def experts(tokens, gain, router, chosen, up, down):
+    legs, rows, width = tokens.shape
+    wide = width + LANES
     vmem = pl.BlockSpec(memory_space=pltpu.VMEM)
     anywhere = pl.BlockSpec(memory_space=pl.ANY)
     copies = 88
     return pl.pallas_call(
         kernel,
-        out_shape=jax.ShapeDtypeStruct(tokens.shape, jnp.bfloat16),
-        in_specs=[vmem, vmem, anywhere, anywhere],
-        out_specs=vmem,
+        out_shape=[jax.ShapeDtypeStruct(tokens.shape, jnp.bfloat16)] * 2,
+        in_specs=[vmem, vmem, vmem, vmem, anywhere, anywhere],
+        out_specs=[vmem, vmem],
         scratch_shapes=[
+            pltpu.VMEM((legs, rows, wide), jnp.bfloat16),
             pltpu.VMEM((RING, CORES, RING, legs, rows, wide), jnp.bfloat16),
             pltpu.VMEM((RING, CORES, RING, legs, rows, width), jnp.bfloat16),
             pltpu.VMEM((RING, RING, legs, rows, width), jnp.bfloat16),
@@ -294,7 +317,6 @@
             pltpu.VMEM((2, RING, legs, rows, width), jnp.bfloat16),
             pltpu.VMEM((2, rows, width), jnp.bfloat16),
             pltpu.VMEM((2, legs, rows, width), jnp.bfloat16),
-            pltpu.VMEM(tokens.shape, jnp.bfloat16),
             pltpu.VMEM(tokens.shape, jnp.bfloat16),
             pltpu.VMEM(up.shape, up.dtype),
             pltpu.VMEM(down.shape, down.dtype),
@@ -308,28 +330,24 @@
             collective_id=0, has_side_effects=True, vmem_limit_bytes=66000000
         ),
         name="experts",
-    )(packed, tokens, up, down)
+    )(tokens, gain, router, chosen, up, down)
 
 
 def shards(in_flight, norm_gain, router_weight, up_weight, down_weight, chosen_experts):
-    tokens = in_flight[:, 0]
-    wide = tokens.astype(jnp.float32)
-    scale = lax.rsqrt(jnp.mean(wide * wide, axis=-1, keepdims=True) + 1e-06)
-    normed = (wide * scale * norm_gain.astype(jnp.float32)).astype(jnp.bfloat16)
-    affinity = jax.nn.sigmoid(
-        jnp.einsum("lrd,lde->lre", normed, router_weight[:, 0], preferred_element_type=jnp.float32)
+    rank, ranks = lax.axis_index("pipe"), lax.axis_size("pipe")
+    moved, arrived = experts(
+        in_flight[:, 0],
+        norm_gain[:, 0],
+        router_weight[:, 0].transpose(0, 2, 1),
+        chosen_experts[0, :, 0],
+        up_weight[:, 0],
+        down_weight[:, 0],
     )
-    labels = jnp.arange(EXPERTS, dtype=jnp.int32)
-    picked = jnp.sum(
-        (chosen_experts[0, :, 0, :, :, None] == labels).astype(jnp.float32), axis=2
-    )
-    weighted = affinity * picked
-    gates = weighted / jnp.sum(weighted, axis=-1, keepdims=True)
-    high = gates.astype(jnp.bfloat16)
-    low = (gates - high.astype(jnp.float32)).astype(jnp.bfloat16)
-    empty = jnp.zeros(gates.shape[:2] + (LANES - 2 * EXPERTS,), jnp.bfloat16)
-    packed = jnp.concatenate([normed, high, low, empty], axis=-1)
-    return experts(packed, tokens, up_weight[:, 0], down_weight[:, 0])[:, None]
+    states = [
+        jnp.where(rank == 0, moved[1], arrived[0]),
+        jnp.where(rank == ranks - 1, moved[0], arrived[1]),
+    ]
+    return jnp.stack(states)[:, None]
 
 
 def solution(mesh):

time: 109 us -> 106 us (0.972)
  the two profiles are of different devices: /device:TPU:64 before, /device:TPU:70 now
where the time goes in v4:
time: 106 us
  Pallas kernels  103 us (97%)
  other arithmetic  1.81 us (2%)
  local copies, waits for them, and re-layouts  1.37 us (1%)
    pallas_call x1, Pallas kernels, experts(): pl.pallas_call(kernel, out_shape=[jax.ShapeDtypeStruct(tokens.shape, jnp....  103 us

profile of v4, /device:TPU:70, one launch (start us, length us, event | category | flops | bytes accessed | tf_op | source)
XLA Modules:
  0.0 105.8 jit_solution(8640599166699763381)
XLA Ops:
  0.0 1.4 %copy.7.chosen = s32[2,16,2]{2,1,0:T(8,128)} copy(s32[2,16,2]{1,2,0:T(2,128)} %bitcast.17) | data formatting | bytes 512 | tf_op jit(solution)/shard_map/squeeze | solution.py:342
  1.4 102.6 %experts.1 = (bf16[2,16,3584]{2,1,0:T(8,128)(2,1)}, bf16[2,16,3584]{2,1,0:T(8,128)(2,1)}) custom-call(bf16[2,16,3584]{2,1,0:T(8,128)(2,1)} %bitcast.14, bf16[2,3584]{1,0:T(2,128)(2,1)} %bitcast.16, bf16[2,4,3584]{2,1,0:T(4,128)(2,1)} %bitcast.15, s32[2,16,2]{2,1,0:T(8,128)} %copy.7.chosen, bf16[2,3584,128]{2,1,0:T(8,128)(2,1)} %bitcast.12, ...), custom_call_target="tpu_custom_call" | custom-call | tf_op jit(solution)/shard_map/experts/pallas_call | solution.py:306
  104.0 1.1 %slice_select_fusion.1 = (bf16[1,16,3584]{2,1,0:T(8,128)(2,1)S(1)}, bf16[1,16,3584]{2,1,0:T(8,128)(2,1)S(1)}) fusion(bf16[2,16,3584]{2,1,0:T(8,128)(2,1)} %get-tuple-element.8, bf16[2,16,3584]{2,1,0:T(8,128)(2,1)} %get-tuple-element.7, pred[]{:T(512)S(6)} %eq.6, pred[]{:T(512)S(6)} %eq.7), kind=kLoop, calls=%fused_computation.2 | loop fusion | flops 114688 | bytes 688130 | tf_op jit(solution)/shard_map/jit(_where)/select_n | solution.py:347
  105.1 0.7 maximum_bitcast_fusion

commit v5 on v4

--- a/solution.py
+++ b/solution.py
@@ -138,11 +138,13 @@
 
             return lax.fori_loop(0, width // TILE, tile_body, carry)
 
-        lax.fori_loop(0, LEGS, leg_body, 0)
-        go(("near", dx), part.at[xx, 1 - c], near.at[dx], sib)
+        for leg in range(LEGS):
+            leg_body(leg, 0)
+            go(("near", dx, leg), part.at[xx, 1 - c, :, leg], near.at[dx, :, leg], sib)
 
     def pair(dx):
-        got("near", dx)
+        got("near", dx, 0)
+        got("near", dx, 1)
         xx = turn(x, dx)
 
         def body(zz, carry):
@@ -343,11 +345,8 @@
         up_weight[:, 0],
         down_weight[:, 0],
     )
-    states = [
-        jnp.where(rank == 0, moved[1], arrived[0]),
-        jnp.where(rank == ranks - 1, moved[0], arrived[1]),
-    ]
-    return jnp.stack(states)[:, None]
+    edge = jnp.stack([rank == 0, rank == ranks - 1])[:, None, None]
+    return jnp.where(edge, moved[::-1], arrived)[:, None]
 
 
 def solution(mesh):

time: 106 us -> 105 us (level)
    broadcast_in_dim x1, other arithmetic: 0.71 us -> 1.86 us  [shards(): return jnp.where(edge, moved[::-1], arrived)[:, None]]
    select_n x1 -> x0, other arithmetic: 1.1 us -> none  [shards(): jnp.where(rank == 0, moved[1], arrived[0])]
where the time goes in v5:
time: 105 us
  Pallas kernels  102 us (97%)
  other arithmetic  1.94 us (2%)
  local copies, waits for them, and re-layouts  1.37 us (1%)
    pallas_call x1, Pallas kernels, experts(): pl.pallas_call(kernel, out_shape=[jax.ShapeDtypeStruct(tokens.shape, jnp....  102 us

profile of v5, /device:TPU:70, one launch (start us, length us, event | category | flops | bytes accessed | tf_op | source)
XLA Modules:
  0.0 105.1 jit_solution(1830531594848894779)
XLA Ops:
  0.0 0.1 pad_add_fusion
  0.1 1.4 %copy.7.chosen = s32[2,16,2]{2,1,0:T(8,128)} copy(s32[2,16,2]{1,2,0:T(2,128)} %bitcast.19) | data formatting | bytes 512 | tf_op jit(solution)/shard_map/squeeze | solution.py:344
  1.4 101.8 %experts.1 = (bf16[2,16,3584]{2,1,0:T(8,128)(2,1)}, bf16[2,16,3584]{2,1,0:T(8,128)(2,1)}) custom-call(bf16[2,16,3584]{2,1,0:T(8,128)(2,1)} %bitcast.16, bf16[2,3584]{1,0:T(2,128)(2,1)} %bitcast.18, bf16[2,4,3584]{2,1,0:T(4,128)(2,1)} %bitcast.17, s32[2,16,2]{2,1,0:T(8,128)} %copy.7.chosen, bf16[2,3584,128]{2,1,0:T(8,128)(2,1)} %bitcast.14, ...), custom_call_target="tpu_custom_call" | custom-call | tf_op jit(solution)/shard_map/experts/pallas_call | solution.py:308
  103.2 1.9 %select_bitcast_fusion = bf16[2,1,16,3584]{3,2,1,0:T(8,128)(2,1)} fusion(bf16[2,16,3584]{2,1,0:T(8,128)(2,1)} %get-tuple-element.8, bf16[2,16,3584]{2,1,0:T(8,128)(2,1)} %get-tuple-element.7, pred[2]{0:T(512)(128)(4,1)S(1)} %pad_add_fusion), kind=kLoop, calls=%fused_computation | loop fusion | flops 114688 | bytes 688130 | tf_op jit(solution)/shard_map/broadcast_in_dim | solution.py:349
